TPU v7x, 32 devices: a whole 2x2x4 slice. The times are simulated.
32 devices in a mesh: rep: 4 (over x, core), row: 4 (over z), col: 2 (over y).
Axes of the slice: x: 2, y: 2, z: 4, core: 2. Of those that a mesh axis runs over, the one named last changes fastest.
Arguments:
- inputs: bfloat16 [4, 128, 6144], P('rep', 'col', 'row'), may hold values from -6 to 6
- w_in: bfloat16 [6144, 24576], P('row', ('rep', 'col')), may hold values from -0.078125 to 0.078125
- w_out: bfloat16 [24576, 6144], P(('rep', 'col'), 'row'), may hold values from -0.0390625 to 0.0390625
- cotangent: bfloat16 [4, 128, 6144], P('rep', 'col', 'row'), may hold values from -1536 to 1536
- counts: int32 [4], replicated, may hold values from 0 to 4, as said below
Outputs:
- block_output: bfloat16 [4, 128, 6144], P('rep', 'col', 'row')
- input_grad: bfloat16 [4, 128, 6144], P('rep', 'col', 'row')
- w_in_grad: float32 [6144, 24576], P('row', ('rep', 'col'))
- w_out_grad: float32 [24576, 6144], P(('rep', 'col'), 'row')
Inputs may be any that keep to these rules, and one draw needn't show every extreme that they name: Replica r completed its first counts[r] micro-batches; at least one replica completed all 4.
All inputs are finite; a program needn't handle non-finite values.
Results may differ from a plain program's by a relative error of at most 0.015.
Values may be sent and summed in bfloat16 or wider, within the bound.
A program may use at most 192 MiB of HBM per device.

v0:
```python
import jax
import jax.numpy as jnp
from jax import lax
from jax.sharding import PartitionSpec as P

MBT = 32


root_coef = 0.7978845608028654
cubic_coef = 0.044715


def gelu_tanh(values):
    inner = root_coef * (values + cubic_coef * values * values * values)
    return 0.5 * values * (1.0 + jnp.tanh(inner))


def gelu_slope(values):
    inner = root_coef * (values + cubic_coef * values * values * values)
    tangent = jnp.tanh(inner)
    return 0.5 * (1.0 + tangent) + 0.5 * values * (1.0 - tangent * tangent) * root_coef * (
        1.0 + 3.0 * cubic_coef * values * values
    )


def right_product(left, right):
    return lax.dot_general(
        left, right, (((1,), (1,)), ((), ())), preferred_element_type=jnp.float32
    )


def first_product(left, right):
    return lax.dot_general(
        left, right, (((0,), (0,)), ((), ())), preferred_element_type=jnp.float32
    )


def body(inputs, w_in, w_out, cotangent, counts):
    rows_local = inputs.shape[1]
    width_local = inputs.shape[2]
    tokens_local = inputs.reshape(rows_local, width_local)
    replicas = lax.axis_size("rep")
    replica_index = lax.axis_index("rep")
    column_index = lax.axis_index("col")
    own_count = jnp.sum(jnp.where(jnp.arange(replicas) == replica_index, counts, 0))
    token_total = (MBT * jnp.sum(counts)).astype(jnp.float32)
    positions = column_index * rows_local + jnp.arange(rows_local, dtype=jnp.int32)
    kept_mask = (positions // MBT < own_count).astype(jnp.float32)
    scaled = (
        cotangent.reshape(rows_local, width_local).astype(jnp.float32)
        * kept_mask[:, None]
        / token_total
    ).astype(jnp.bfloat16)
    tokens_all, scaled_all = (
        lax.all_gather(tokens_local, "col", axis=0, tiled=True),
        lax.all_gather(scaled, "col", axis=0, tiled=True),
    )
    inner_cols = lax.all_gather(w_in, "rep", axis=1, tiled=True)
    outer_rows = lax.all_gather(w_out, "rep", axis=0, tiled=True)
    partial_hidden = jnp.dot(tokens_all, inner_cols, preferred_element_type=jnp.float32)
    hidden = lax.psum_scatter(
        partial_hidden.astype(jnp.bfloat16), "row", scatter_dimension=0, tiled=True
    ).astype(jnp.float32)
    active_share = gelu_tanh(hidden).astype(jnp.bfloat16)
    activated = lax.all_gather(active_share, "row", axis=0, tiled=True)
    output_terms = jnp.dot(activated, outer_rows, preferred_element_type=jnp.float32)
    output_local = lax.psum_scatter(
        output_terms.astype(jnp.bfloat16), "col", scatter_dimension=0, tiled=True
    ).astype(jnp.float32)
    block_output = (tokens_local.astype(jnp.float32) + output_local).astype(jnp.bfloat16)
    slope_terms = right_product(scaled_all, outer_rows)
    slope_sum = lax.psum_scatter(
        slope_terms.astype(jnp.bfloat16), "row", scatter_dimension=0, tiled=True
    ).astype(jnp.float32)
    grad_share = (slope_sum * gelu_slope(hidden)).astype(jnp.bfloat16)
    hidden_grad = lax.all_gather(grad_share, "row", axis=0, tiled=True)
    back_terms = right_product(hidden_grad, inner_cols)
    back_local = lax.psum_scatter(
        back_terms.astype(jnp.bfloat16), "col", scatter_dimension=0, tiled=True
    ).astype(jnp.float32)
    input_grad = (scaled.astype(jnp.float32) + back_local).astype(jnp.bfloat16)
    token_reps, scaled_reps = (
        lax.all_gather(tokens_all, "rep", axis=0, tiled=True),
        lax.all_gather(scaled_all, "rep", axis=0, tiled=True),
    )
    hidden_reps, active_reps = (
        lax.all_to_all(hidden_grad, "rep", split_axis=1, concat_axis=0, tiled=True),
        lax.all_to_all(activated, "rep", split_axis=1, concat_axis=0, tiled=True),
    )
    w_in_grad = first_product(token_reps, hidden_reps)
    w_out_grad = first_product(active_reps, scaled_reps)
    return (
        block_output.reshape(1, rows_local, width_local),
        input_grad.reshape(1, rows_local, width_local),
        w_in_grad,
        w_out_grad,
    )


def solution(mesh):
    placed = (
        P("rep", "col", "row"),
        P("row", ("rep", "col")),
        P(("rep", "col"), "row"),
        P("rep", "col", "row"),
        P(),
    )
    return jax.shard_map(
        body,
        mesh=mesh,
        in_specs=placed,
        out_specs=(
            P("rep", "col", "row"),
            P("rep", "col", "row"),
            P("row", ("rep", "col")),
            P(("rep", "col"), "row"),
        ),
        check_vma=False,
    )
```

profile of v0, /device:TPU:0, one launch (start us, length us, event | category | flops | bytes accessed | tf_op | source)
XLA Modules:
  0.0 861.8 jit_solution(15907317632032920485)
XLA Ops:
  7.2 0.0 all-gather.9.cloned.1.call-start
  7.2 0.7 all-gather.9.cloned.1.call-update
  7.9 0.0 copy-start.6
  7.9 0.0 all-gather.13.cloned.1.call-start
  8.0 0.7 all-gather.13.cloned.1.call-update
  8.7 0.0 reduce-scatter.5.cloned.1.call-start
  8.7 0.1 copy-done.6
  8.8 8.5 all-gather
  17.4 0.0 copy-start.2
  17.4 222.1 %all-gather.9.cloned.1.call-done = bf16[1536,12288]{1,0:T(8,128)(2,1)} async-done(((bf16[1536,3072]{1,0:T(8,128)(2,1)}), bf16[1536,12288]{1,0:T(8,128)(2,1)}) %all-gather.9.cloned.1.call-update) | async-done | bytes 37748752 | tf_op jit(solution)/shard_map/all_gather | solution.py:58
  239.5 20.2 %convolution_convert_fusion.1 = bf16[128,12288]{1,0:T(8,128)(2,1)} fusion(bf16[1536,12288]{1,0:T(8,128)(2,1)} %all-gather.9.cloned.1.call-done, bf16[1,128,1536]{2,1,0:T(8,128)(2,1)S(1)} %all-gather), kind=kOutput, calls=%fused_computation.1 | convolution fusion | flops 4833411072 | bytes 41287680 | tf_op jit(solution)/shard_map/dot_general | solution.py:60
  259.6 0.0 copy-done.2
  259.6 0.0 copy-start.8
  259.6 0.0 copy-start.4
  259.6 0.0 reduce-scatter.5.cloned.1.call-update
  259.7 0.0 reduce-scatter.9.cloned.1.call-start
  259.7 0.6 copy-done.8
  260.3 0.6 fusion.18
  261.6 0.7 compare_convert_fusion
  262.3 0.0 copy-done.4
  262.3 0.1 fusion.13
  262.4 7.7 all_gather.28
  270.1 0.0 copy-start.3
  270.1 198.2 %all-gather.13.cloned.1.call-done = bf16[12288,1536]{1,0:T(8,128)(2,1)} async-done(((bf16[3072,1536]{1,0:T(8,128)(2,1)}), bf16[12288,1536]{1,0:T(8,128)(2,1)}) %all-gather.13.cloned.1.call-update) | async-done | bytes 37748752 | tf_op jit(solution)/shard_map/all_gather | solution.py:59
  468.3 19.7 %convolution_convert_fusion = bf16[128,12288]{1,0:T(8,128)(2,1)} fusion(bf16[128,1536]{1,0:T(8,128)(2,1)S(1)} %all_gather.28, bf16[12288,1536]{1,0:T(8,128)(2,1)} %all-gather.13.cloned.1.call-done), kind=kOutput, calls=%fused_computation | convolution fusion | flops 4833411072 | bytes 41287680 | tf_op jit(solution)/shard_map/dot_general | solution.py:27
  488.0 0.0 copy-done.3
  488.0 0.0 reduce-scatter.9.cloned.1.call-update
  488.0 0.0 all-gather.11.cloned.1.call-start
  488.1 43.5 %reduce-scatter.5.cloned.1.call-done = bf16[32,12288]{1,0:T(8,128)(2,1)} async-done(((bf16[128,12288]{1,0:T(8,128)(2,1)}), bf16[32,12288]{1,0:T(8,128)(2,1)}) %reduce-scatter.5.cloned.1.call-update) | async-done | bytes 786448 | tf_op jit(solution)/shard_map/reduce_scatter | solution.py:61
  531.6 63.0 %reduce-scatter.9.cloned.1.call-done = bf16[32,12288]{1,0:T(8,128)(2,1)} async-done(((bf16[128,12288]{1,0:T(8,128)(2,1)}), bf16[32,12288]{1,0:T(8,128)(2,1)}) %reduce-scatter.9.cloned.1.call-update) | async-done | bytes 786448 | tf_op jit(solution)/shard_map/reduce_scatter | solution.py:72
  594.6 3.7 fusion.7
  598.3 0.0 all-gather.11.cloned.1.call-update
  598.3 0.0 all-gather.15.cloned.1.call-start
  598.4 0.5 all-gather.15.cloned.1.call-update
  598.9 0.0 reduce-scatter.7.cloned.1.call-start
  599.0 62.9 %all-gather.11.cloned.1.call-done = bf16[128,12288]{1,0:T(8,128)(2,1)} async-done(((bf16[32,12288]{1,0:T(8,128)(2,1)}), bf16[128,12288]{1,0:T(8,128)(2,1)}) %all-gather.11.cloned.1.call-update) | async-done | bytes 3145744 | tf_op jit(solution)/shard_map/all_gather | solution.py:65
  661.9 16.8 %convolution_convert_fusion.3 = bf16[128,1536]{1,0:T(8,128)(2,1)} fusion(bf16[128,12288]{1,0:T(8,128)(2,1)} %all-gather.11.cloned.1.call-done, bf16[12288,1536]{1,0:T(8,128)(2,1)} %all-gather.13.cloned.1.call-done), kind=kOutput, calls=%fused_computation.13 | convolution fusion | flops 4832034816 | bytes 41287680 | tf_op jit(solution)/shard_map/dot_general | solution.py:66
  678.6 0.0 reduce-scatter.7.cloned.1.call-update
  678.7 0.2 reduce-scatter.11.cloned.1.call-start
  678.9 47.1 %all-gather.15.cloned.1.call-done = bf16[128,12288]{1,0:T(8,128)(2,1)} async-done(((bf16[32,12288]{1,0:T(8,128)(2,1)}), bf16[128,12288]{1,0:T(8,128)(2,1)}) %all-gather.15.cloned.1.call-update) | async-done | bytes 3145744 | tf_op jit(solution)/shard_map/all_gather | solution.py:76
  726.0 0.0 copy-start
  726.0 23.0 %convolution_convert_fusion.2 = bf16[128,1536]{1,0:T(8,128)(2,1)} fusion(bf16[128,12288]{1,0:T(8,128)(2,1)} %all-gather.15.cloned.1.call-done, bf16[1536,12288]{1,0:T(8,128)(2,1)} %all-gather.9.cloned.1.call-done), kind=kOutput, calls=%fused_computation.12 | convolution fusion | flops 4832034816 | bytes 41287680 | tf_op jit(solution)/shard_map/dot_general | solution.py:27
  749.0 0.0 reduce-scatter.11.cloned.1.call-update
  749.0 0.0 all-gather.19.cloned.1.call-start
  749.1 0.7 all-gather.19.cloned.1.call-update
  749.8 0.0 copy-done
  749.8 1.9 copy.18
  751.7 0.0 copy-start.1
  751.7 4.9 all-to-all-start
  756.6 0.0 all-gather.17.cloned.1.call-start
  756.7 0.5 all-gather.17.cloned.1.call-update
  757.2 0.0 copy-done.1
  757.2 1.9 copy.17
  759.2 42.9 %all-to-all-done = bf16[128,4,3072]{2,0,1:T(8,128)(2,1)} async-done(((bf16[128,4,3072]{2,0,1:T(8,128)(2,1)}), bf16[128,4,3072]{2,0,1:T(8,128)(2,1)}, u32[]{:S(2)}, u32[]{:S(2)}) %all-to-all-start) | async-done | bytes 3145760 | tf_op jit(solution)/shard_map/all_to_all | solution.py:87
  802.0 3.8 all-to-all-start.1
  805.9 0.0 reduce-scatter.7.cloned.1.call-done
  805.9 0.0 copy-done.7
  805.9 1.7 fusion.17
  807.6 0.0 copy-done.5
  807.6 1.7 fusion.16
  809.3 11.4 %convolution_bitcast_fusion = f32[1536,3072]{0,1:T(8,128)} fusion(bf16[512,3072]{1,0:T(8,128)(2,1)} %bitcast.6, bf16[1,512,1536]{2,1,0:T(8,128)(2,1)} %all-gather.19.cloned.1.call-done), kind=kOutput, calls=%fused_computation.2 | convolution fusion | flops 4831838208 | bytes 23592960 | tf_op jit(solution)/shard_map/dot_general | solution.py:33
  820.7 18.6 %copy.12 = f32[1536,3072]{1,0:T(8,128)} copy(f32[1536,3072]{0,1:T(8,128)} %convolution_bitcast_fusion) | data formatting | bytes 37748736
  839.3 4.7 all-to-all-done.1
  844.1 10.9 %fusion.19 = f32[3072,1536]{1,0:T(8,128)} fusion(bf16[512,3072]{1,0:T(8,128)(2,1)S(1)} %bitcast.48, bf16[512,1536]{1,0:T(8,128)(2,1)} %all-gather.17.cloned.1.call-done), kind=kOutput, calls=%fused_computation.42 | convolution fusion | flops 4831838208 | bytes 23592960 | tf_op jit(solution)/shard_map/dot_general | solution.py:33
  (5 shorter events, 0.0 us)
Async XLA Ops:
  7.2 232.3 %all-gather.9.cloned.1.call-start = ((), (), s32[]{:S(2)}) async-start(), calls=%async_computation.6 | async-start | bytes 47185920 | tf_op jit(solution)/shard_map/all_gather | solution.py:58
  7.9 0.9 copy-start.6
  7.9 460.3 %all-gather.13.cloned.1.call-start = ((), (), s32[]{:S(2)}) async-start(), calls=%async_computation.9 | async-start | bytes 47185920 | tf_op jit(solution)/shard_map/all_gather | solution.py:59
  8.7 522.9 %reduce-scatter.5.cloned.1.call-start = ((), (), s32[]{:S(2)}) async-start(), calls=%async_computation.7 | async-start | bytes 3932160 | tf_op jit(solution)/shard_map/reduce_scatter | solution.py:61
  17.4 242.3 %copy-start.2 = (bf16[1,128,1536]{2,1,0:T(8,128)(2,1)}, bf16[1,128,1536]{2,1,0:T(8,128)(2,1)S(1)}, u32[]{:S(2)}) copy-start(bf16[1,128,1536]{2,1,0:T(8,128)(2,1)S(1)} %all-gather) | copy-start | bytes 1179652
  259.6 0.7 copy-start.8
  259.6 2.6 copy-start.4
  259.7 335.0 %reduce-scatter.9.cloned.1.call-start = ((), (), s32[]{:S(2)}) async-start(), calls=%async_computation.11 | async-start | bytes 3932160 | tf_op jit(solution)/shard_map/reduce_scatter | solution.py:72
  270.1 217.9 %copy-start.3 = (bf16[128,1536]{1,0:T(8,128)(2,1)}, bf16[128,1536]{1,0:T(8,128)(2,1)S(1)}, u32[]{:S(2)}) copy-start(bf16[128,1536]{1,0:T(8,128)(2,1)S(1)} %all_gather.28) | copy-start | bytes 1179652
  488.0 173.8 %all-gather.11.cloned.1.call-start = ((), (), s32[]{:S(2)}) async-start(), calls=%async_computation.8 | async-start | bytes 3932160 | tf_op jit(solution)/shard_map/all_gather | solution.py:65
  598.3 127.6 %all-gather.15.cloned.1.call-start = ((), (), s32[]{:S(2)}) async-start(), calls=%async_computation.12 | async-start | bytes 3932160 | tf_op jit(solution)/shard_map/all_gather | solution.py:76
  598.9 207.0 %reduce-scatter.7.cloned.1.call-start = ((), (), s32[]{:S(2)}) async-start(), calls=%async_computation.10 | async-start | bytes 589824 | tf_op jit(solution)/shard_map/reduce_scatter | solution.py:67
  678.7 128.9 %reduce-scatter.11.cloned.1.call-start = ((), (), s32[]{:S(2)}) async-start(), calls=%async_computation.13 | async-start | bytes 589824 | tf_op jit(solution)/shard_map/reduce_scatter | solution.py:78
  726.0 23.8 %copy-start = (bf16[128,12288]{1,0:T(8,128)(2,1)S(1)}, bf16[128,12288]{1,0:T(8,128)(2,1)}, u32[]{:S(2)}) copy-start(bf16[128,12288]{1,0:T(8,128)(2,1)} %all-gather.15.cloned.1.call-done) | copy-start | bytes 9437188
  749.0 60.3 %all-gather.19.cloned.1.call-start = ((), (), s32[]{:S(2)}) async-start(), calls=%async_computation.15 | async-start | bytes 1966080 | tf_op jit(solution)/shard_map/all_gather | solution.py:83
  751.7 5.5 copy-start.1
  751.7 50.3 %all-to-all-start = ((bf16[128,4,3072]{2,0,1:T(8,128)(2,1)}), bf16[128,4,3072]{2,0,1:T(8,128)(2,1)}, u32[]{:S(2)}, u32[]{:S(2)}) async-start(bf16[128,4,3072]{2,0,1:T(8,128)(2,1)} %bitcast.47), calls=%async_computation.4 | async-start | bytes 6291456 | tf_op jit(solution)/shard_map/all_to_all | solution.py:87
  756.6 82.7 %all-gather.17.cloned.1.call-start = ((), (), s32[]{:S(2)}) async-start(), calls=%async_computation.14 | async-start | bytes 1966080 | tf_op jit(solution)/shard_map/all_gather | solution.py:84
  802.0 3.9 copy-start.7
  802.0 5.5 copy-start.5
  802.0 42.0 %all-to-all-start.1 = ((bf16[128,4,3072]{2,0,1:T(8,128)(2,1)}), bf16[128,4,3072]{2,0,1:T(8,128)(2,1)S(1)}, u32[]{:S(2)}, u32[]{:S(2)}) async-start(bf16[128,4,3072]{2,0,1:T(8,128)(2,1)} %bitcast.46), calls=%async_computation.5 | async-start | bytes 6291456 | tf_op jit(solution)/shard_map/all_to_all | solution.py:88
Sparse Core Ops, SparseCore 0:
  9.5 229.8 all-gather.8
  241.0 227.1 all-gather.12
  471.1 60.4 reduce-scatter.4
  534.3 60.2 reduce-scatter.8
  598.5 63.3 all-gather.10
  663.9 62.0 all-gather.14
  728.8 11.8 reduce-scatter.6
  749.1 11.8 reduce-scatter.10
  762.6 28.1 all-gather.18
  792.2 21.0 all-gather.16
where the time goes:
time: 863 us; the launch traced here: 862 us
  waiting for transfers between devices  688 us (80%)
  matrix products  102 us (12%)
  local copies, waits for them, and re-layouts  23.2 us (3%)
  blocking collectives  16.2 us (2%)
  between operations  14.9 us (2%)
  starting transfers between devices  9.32 us (1%)
    all_gather x1, waiting for transfers between devices, body(): inner_cols = lax.all_gather(w_in, 'rep', axis=1, tiled=True)  222 us
    all_gather x1, waiting for transfers between devices, body(): outer_rows = lax.all_gather(w_out, 'rep', axis=0, tiled=True)  198 us
    reduce_scatter x1, waiting for transfers between devices, body(): lax.psum_scatter(slope_terms.astype(jnp.bfloat16), 'row', scatter_dimensi...  63 us
    all_gather x1, waiting for transfers between devices, body(): activated = lax.all_gather(active_share, 'row', axis=0, tiled=True)  62.9 us
    all_gather x1, waiting for transfers between devices, body(): hidden_grad = lax.all_gather(grad_share, 'row', axis=0, tiled=True)  47.1 us
    reduce_scatter x1, waiting for transfers between devices, body(): lax.psum_scatter(partial_hidden.astype(jnp.bfloat16), 'row', scatter_dime...  43.5 us
    all_to_all x1, waiting for transfers between devices, body(): lax.all_to_all(hidden_grad, 'rep', split_axis=1, concat_axis=0, tiled=True)  42.9 us
    dot_general x2, matrix products, right_product(): lax.dot_general(left, right, (((1,), (1,)), ((), ())), preferred_element_...  42.8 us
  transfers between devices with their start and end apart: 12, of which 8 were waited for; matrix products, arithmetic and copies ran while one was open for 14% of the time, Pallas kernels for 0%

commit v1 on v0

--- a/solution.py
+++ b/solution.py
@@ -51,44 +51,32 @@
         * kept_mask[:, None]
         / token_total
     ).astype(jnp.bfloat16)
-    tokens_all, scaled_all = (
-        lax.all_gather(tokens_local, "col", axis=0, tiled=True),
-        lax.all_gather(scaled, "col", axis=0, tiled=True),
-    )
-    inner_cols = lax.all_gather(w_in, "rep", axis=1, tiled=True)
-    outer_rows = lax.all_gather(w_out, "rep", axis=0, tiled=True)
-    partial_hidden = jnp.dot(tokens_all, inner_cols, preferred_element_type=jnp.float32)
+    tokens_all = lax.all_gather(tokens_local, ("rep", "col"), axis=0, tiled=True)
+    scaled_all = lax.all_gather(scaled, ("rep", "col"), axis=0, tiled=True)
+    partial_hidden = jnp.dot(tokens_all, w_in, preferred_element_type=jnp.float32)
     hidden = lax.psum_scatter(
         partial_hidden.astype(jnp.bfloat16), "row", scatter_dimension=0, tiled=True
     ).astype(jnp.float32)
-    active_share = gelu_tanh(hidden).astype(jnp.bfloat16)
-    activated = lax.all_gather(active_share, "row", axis=0, tiled=True)
-    output_terms = jnp.dot(activated, outer_rows, preferred_element_type=jnp.float32)
-    output_local = lax.psum_scatter(
-        output_terms.astype(jnp.bfloat16), "col", scatter_dimension=0, tiled=True
-    ).astype(jnp.float32)
-    block_output = (tokens_local.astype(jnp.float32) + output_local).astype(jnp.bfloat16)
-    slope_terms = right_product(scaled_all, outer_rows)
+    slope_terms = right_product(scaled_all, w_out)
     slope_sum = lax.psum_scatter(
         slope_terms.astype(jnp.bfloat16), "row", scatter_dimension=0, tiled=True
     ).astype(jnp.float32)
+    active_share = gelu_tanh(hidden).astype(jnp.bfloat16)
+    activated = lax.all_gather(active_share, "row", axis=0, tiled=True)
     grad_share = (slope_sum * gelu_slope(hidden)).astype(jnp.bfloat16)
     hidden_grad = lax.all_gather(grad_share, "row", axis=0, tiled=True)
-    back_terms = right_product(hidden_grad, inner_cols)
+    output_terms = jnp.dot(activated, w_out, preferred_element_type=jnp.float32)
+    output_local = lax.psum_scatter(
+        output_terms.astype(jnp.bfloat16), ("rep", "col"), scatter_dimension=0, tiled=True
+    ).astype(jnp.float32)
+    block_output = (tokens_local.astype(jnp.float32) + output_local).astype(jnp.bfloat16)
+    w_out_grad = first_product(activated, scaled_all)
+    back_terms = right_product(hidden_grad, w_in)
     back_local = lax.psum_scatter(
-        back_terms.astype(jnp.bfloat16), "col", scatter_dimension=0, tiled=True
+        back_terms.astype(jnp.bfloat16), ("rep", "col"), scatter_dimension=0, tiled=True
     ).astype(jnp.float32)
     input_grad = (scaled.astype(jnp.float32) + back_local).astype(jnp.bfloat16)
-    token_reps, scaled_reps = (
-        lax.all_gather(tokens_all, "rep", axis=0, tiled=True),
-        lax.all_gather(scaled_all, "rep", axis=0, tiled=True),
-    )
-    hidden_reps, active_reps = (
-        lax.all_to_all(hidden_grad, "rep", split_axis=1, concat_axis=0, tiled=True),
-        lax.all_to_all(activated, "rep", split_axis=1, concat_axis=0, tiled=True),
-    )
-    w_in_grad = first_product(token_reps, hidden_reps)
-    w_out_grad = first_product(active_reps, scaled_reps)
+    w_in_grad = first_product(tokens_all, hidden_grad)
     return (
         block_output.reshape(1, rows_local, width_local),
         input_grad.reshape(1, rows_local, width_local),

time: 863 us -> 416 us (0.48)
  waiting for transfers between devices: 688 us -> 309 us
  matrix products: 102 us -> 61.2 us
  blocking collectives: 16.2 us -> 0 us
  starting transfers between devices: 9.32 us -> 0.5 us
    all_gather x4 -> x2, waiting for transfers between devices: 420 us -> 45.8 us  [the longest x1 27.6 us: body(): scaled_all = lax.all_gather(scaled, ('rep', 'col'), axis=0, tiled=True)]
    all_to_all x2 -> x0, waiting for transfers between devices: 47.6 us -> none  [the longest x1 42.9 us: body(): lax.all_to_all(hidden_grad, 'rep', split_axis=1, concat_axis=0, tiled=True)]
    reduce_scatter x2, waiting for transfers between devices: 0.02 us -> 28.8 us  [the longest x1 28.8 us: body(): lax.psum_scatter(back_terms.astype(jnp.bfloat16), ('rep', 'col'), scatter...]
    dot_general x2, matrix products: 42.8 us -> 19.7 us  [right_product(): lax.dot_general(left, right, (((1,), (1,)), ((), ())), preferred_element_...]
    reduce_scatter x1, waiting for transfers between devices: 43.5 us -> 63.1 us  [body(): lax.psum_scatter(partial_hidden.astype(jnp.bfloat16), 'row', scatter_dime...]
    dot_general x2, matrix products: 36.9 us -> 19.5 us  [the longest x1 10.3 us: body(): output_terms = jnp.dot(activated, w_out, preferred_element_type=jnp.float32)]
    all_gather x2 -> x0, blocking collectives: 16.2 us -> none  [the longest x1 8.54 us: body(): lax.all_gather(tokens_local, 'col', axis=0, tiled=True)]
    reduce_scatter x1, waiting for transfers between devices: 63 us -> 54 us  [body(): lax.psum_scatter(slope_terms.astype(jnp.bfloat16), 'row', scatter_dimensi...]
  transfers between devices with their start and end apart: 12 -> 8, of which waited for: 8 -> 7; matrix products, arithmetic and copies ran while one was open for 14% -> 20% of each run, Pallas kernels for 0% -> 0%
where the time goes in v1:
time: 416 us
  waiting for transfers between devices  309 us (74%)
  matrix products  61.2 us (15%)
  local copies, waits for them, and re-layouts  19 us (5%)
  between operations  14.8 us (4%)
  other arithmetic  10.8 us (3%)
    reduce_scatter x1, waiting for transfers between devices, body(): lax.psum_scatter(partial_hidden.astype(jnp.bfloat16), 'row', scatter_dime...  63.1 us
    all_gather x1, waiting for transfers between devices, body(): activated = lax.all_gather(active_share, 'row', axis=0, tiled=True)  62.9 us
    reduce_scatter x1, waiting for transfers between devices, body(): lax.psum_scatter(slope_terms.astype(jnp.bfloat16), 'row', scatter_dimensi...  54 us
    all_gather x1, waiting for transfers between devices, body(): hidden_grad = lax.all_gather(grad_share, 'row', axis=0, tiled=True)  53.6 us
    reduce_scatter x1, waiting for transfers between devices, body(): lax.psum_scatter(back_terms.astype(jnp.bfloat16), ('rep', 'col'), scatter...  28.8 us
    all_gather x1, waiting for transfers between devices, body(): scaled_all = lax.all_gather(scaled, ('rep', 'col'), axis=0, tiled=True)  27.6 us
    dot_general x2, matrix products, first_product(): lax.dot_general(left, right, (((0,), (0,)), ((), ())), preferred_element_...  22 us
    dot_general x2, matrix products, right_product(): lax.dot_general(left, right, (((1,), (1,)), ((), ())), preferred_element_...  19.7 us
  transfers between devices with their start and end apart: 8, of which 7 were waited for; matrix products, arithmetic and copies ran while one was open for 20% of the time, Pallas kernels for 0%

profile of v1, /device:TPU:0, one launch (start us, length us, event | category | flops | bytes accessed | tf_op | source)
XLA Modules:
  0.0 415.8 jit_solution(2729077798957875447)
XLA Ops:
  7.2 0.0 all-gather.8.cloned.1.call-start
  7.2 1.3 fusion.18
  9.2 0.7 compare_convert_fusion
  9.8 1.7 fusion.14
  11.6 0.0 all-gather.8.cloned.1.call-update
  11.6 0.0 all-gather.12.cloned.1.call-start
  11.6 0.7 all-gather.12.cloned.1.call-update
  12.3 0.0 reduce-scatter.9.cloned.1.call-start
  12.4 27.6 %all-gather.8.cloned.1.call-done = bf16[512,1536]{1,0:T(8,128)(2,1)} async-done(((bf16[64,1536]{1,0:T(8,128)(2,1)}), bf16[512,1536]{1,0:T(8,128)(2,1)}) %all-gather.8.cloned.1.call-update) | async-done | bytes 1572880 | tf_op jit(solution)/shard_map/all_gather | solution.py:55
  40.0 9.3 %convolution_convert_fusion = bf16[512,3072]{1,0:T(8,128)(2,1)} fusion(bf16[512,1536]{1,0:T(8,128)(2,1)} %all-gather.8.cloned.1.call-done, bf16[3072,1536]{1,0:T(8,128)(2,1)} %param.7), kind=kOutput, calls=%fused_computation.1 | convolution fusion | flops 4833411072 | bytes 14155776 | tf_op jit(solution)/shard_map/dot_general | solution.py:27
  49.3 0.0 reduce-scatter.9.cloned.1.call-update
  49.3 0.0 reduce-scatter.5.cloned.1.call-start
  49.4 18.1 %all-gather.12.cloned.1.call-done = bf16[1,512,1536]{2,1,0:T(8,128)(2,1)} async-done(((bf16[1,64,1536]{2,1,0:T(8,128)(2,1)}), bf16[1,512,1536]{2,1,0:T(8,128)(2,1)}) %all-gather.12.cloned.1.call-update) | async-done | bytes 1572880 | tf_op jit(solution)/shard_map/all_gather | solution.py:54
  67.5 9.2 %convolution_convert_fusion.1 = bf16[512,3072]{1,0:T(8,128)(2,1)} fusion(bf16[1536,3072]{1,0:T(8,128)(2,1)} %param.6, bf16[1,512,1536]{2,1,0:T(8,128)(2,1)} %all-gather.12.cloned.1.call-done), kind=kOutput, calls=%fused_computation.2 | convolution fusion | flops 4833411072 | bytes 14155776 | tf_op jit(solution)/shard_map/dot_general | solution.py:56
  76.7 0.0 reduce-scatter.5.cloned.1.call-update
  76.7 0.0 all-gather.6.cloned.1.call-start
  76.8 54.0 %reduce-scatter.9.cloned.1.call-done = bf16[128,3072]{1,0:T(8,128)(2,1)} async-done(((bf16[512,3072]{1,0:T(8,128)(2,1)}), bf16[128,3072]{1,0:T(8,128)(2,1)}) %reduce-scatter.9.cloned.1.call-update) | async-done | bytes 786448 | tf_op jit(solution)/shard_map/reduce_scatter | solution.py:61
  130.8 63.1 %reduce-scatter.5.cloned.1.call-done = bf16[128,3072]{1,0:T(8,128)(2,1)} async-done(((bf16[512,3072]{1,0:T(8,128)(2,1)}), bf16[128,3072]{1,0:T(8,128)(2,1)}) %reduce-scatter.5.cloned.1.call-update) | async-done | bytes 786448 | tf_op jit(solution)/shard_map/reduce_scatter | solution.py:57
  193.9 3.7 fusion.7
  197.6 0.0 all-gather.6.cloned.1.call-update
  197.6 0.0 all-gather.10.cloned.1.call-start
  197.7 0.5 all-gather.10.cloned.1.call-update
  198.2 0.0 reduce-scatter.7.cloned.1.call-start
  198.2 62.9 %all-gather.6.cloned.1.call-done = bf16[512,3072]{1,0:T(8,128)(2,1)} async-done(((bf16[128,3072]{1,0:T(8,128)(2,1)}), bf16[512,3072]{1,0:T(8,128)(2,1)}) %all-gather.6.cloned.1.call-update) | async-done | bytes 3145744 | tf_op jit(solution)/shard_map/all_gather | solution.py:65
  261.1 10.3 %convolution_convert_fusion.3 = bf16[512,1536]{1,0:T(8,128)(2,1)} fusion(bf16[512,3072]{1,0:T(8,128)(2,1)} %all-gather.6.cloned.1.call-done, bf16[3072,1536]{1,0:T(8,128)(2,1)} %param.7), kind=kOutput, calls=%fused_computation.11 | convolution fusion | flops 4832624640 | bytes 14155776 | tf_op jit(solution)/shard_map/dot_general | solution.py:68
  271.4 0.0 reduce-scatter.7.cloned.1.call-update
  271.4 0.2 reduce-scatter.11.cloned.1.call-start
  271.6 53.6 %all-gather.10.cloned.1.call-done = bf16[512,3072]{1,0:T(8,128)(2,1)} async-done(((bf16[128,3072]{1,0:T(8,128)(2,1)}), bf16[512,3072]{1,0:T(8,128)(2,1)}) %all-gather.10.cloned.1.call-update) | async-done | bytes 3145744 | tf_op jit(solution)/shard_map/all_gather | solution.py:67
  325.2 0.0 copy-start.3
  325.2 10.5 %convolution_convert_fusion.2 = bf16[512,1536]{1,0:T(8,128)(2,1)} fusion(bf16[512,3072]{1,0:T(8,128)(2,1)} %all-gather.10.cloned.1.call-done, bf16[1536,3072]{1,0:T(8,128)(2,1)} %param.6), kind=kOutput, calls=%fused_computation.10 | convolution fusion | flops 4832624640 | bytes 14155776 | tf_op jit(solution)/shard_map/dot_general | solution.py:27
  335.7 0.0 reduce-scatter.11.cloned.1.call-update
  335.7 0.0 copy-done.3
  335.7 11.0 %convolution_bitcast_fusion = f32[1536,3072]{0,1:T(8,128)} fusion(bf16[512,3072]{1,0:T(8,128)(2,1)S(1)} %copy-done.3, bf16[1,512,1536]{2,1,0:T(8,128)(2,1)} %all-gather.12.cloned.1.call-done), kind=kOutput, calls=%fused_computation | convolution fusion | flops 4831838208 | bytes 23592960 | tf_op jit(solution)/shard_map/dot_general | solution.py:33
  346.8 0.0 copy-start.2
  346.8 19.0 %copy.9 = f32[1536,3072]{1,0:T(8,128)} copy(f32[1536,3072]{0,1:T(8,128)} %convolution_bitcast_fusion) | data formatting | bytes 37748736
  365.8 0.0 copy-done.2
  365.8 0.0 copy-start
  365.8 0.0 copy-start.1
  365.8 11.0 %fusion.19 = f32[3072,1536]{1,0:T(8,128)} fusion(bf16[512,3072]{1,0:T(8,128)(2,1)S(1)} %copy-done.2, bf16[512,1536]{1,0:T(8,128)(2,1)} %all-gather.8.cloned.1.call-done), kind=kOutput, calls=%fused_computation.40 | convolution fusion | flops 4831838208 | bytes 23592960 | tf_op jit(solution)/shard_map/dot_general | solution.py:33
  376.8 0.0 reduce-scatter.7.cloned.1.call-done
  376.8 0.0 copy-done
  376.8 1.7 fusion.17
  378.4 28.8 %reduce-scatter.11.cloned.1.call-done = bf16[64,1536]{1,0:T(8,128)(2,1)} async-done(((bf16[512,1536]{1,0:T(8,128)(2,1)}), bf16[64,1536]{1,0:T(8,128)(2,1)}) %reduce-scatter.11.cloned.1.call-update) | async-done | bytes 196624 | tf_op jit(solution)/shard_map/reduce_scatter | solution.py:75
  407.2 0.0 copy-done.1
  407.2 1.7 fusion.16
Async XLA Ops:
  7.2 32.9 %all-gather.8.cloned.1.call-start = ((), (), s32[]{:S(2)}) async-start(), calls=%async_computation.7 | async-start | bytes 1769472 | tf_op jit(solution)/shard_map/all_gather | solution.py:55
  11.6 55.9 %all-gather.12.cloned.1.call-start = ((), (), s32[]{:S(2)}) async-start(), calls=%async_computation.11 | async-start | bytes 1769472 | tf_op jit(solution)/shard_map/all_gather | solution.py:54
  12.3 118.5 %reduce-scatter.9.cloned.1.call-start = ((), (), s32[]{:S(2)}) async-start(), calls=%async_computation.8 | async-start | bytes 3932160 | tf_op jit(solution)/shard_map/reduce_scatter | solution.py:61
  49.3 144.6 %reduce-scatter.5.cloned.1.call-start = ((), (), s32[]{:S(2)}) async-start(), calls=%async_computation.4 | async-start | bytes 3932160 | tf_op jit(solution)/shard_map/reduce_scatter | solution.py:57
  76.7 184.4 %all-gather.6.cloned.1.call-start = ((), (), s32[]{:S(2)}) async-start(), calls=%async_computation.5 | async-start | bytes 3932160 | tf_op jit(solution)/shard_map/all_gather | solution.py:65
  197.6 127.6 %all-gather.10.cloned.1.call-start = ((), (), s32[]{:S(2)}) async-start(), calls=%async_computation.9 | async-start | bytes 3932160 | tf_op jit(solution)/shard_map/all_gather | solution.py:67
  198.2 178.6 %reduce-scatter.7.cloned.1.call-start = ((), (), s32[]{:S(2)}) async-start(), calls=%async_computation.6 | async-start | bytes 1769472 | tf_op jit(solution)/shard_map/reduce_scatter | solution.py:69
  271.4 135.8 %reduce-scatter.11.cloned.1.call-start = ((), (), s32[]{:S(2)}) async-start(), calls=%async_computation.10 | async-start | bytes 1769472 | tf_op jit(solution)/shard_map/reduce_scatter | solution.py:75
  325.2 10.5 %copy-start.3 = (bf16[512,3072]{1,0:T(8,128)(2,1)S(1)}, bf16[512,3072]{1,0:T(8,128)(2,1)}, u32[]{:S(2)}) copy-start(bf16[512,3072]{1,0:T(8,128)(2,1)} %all-gather.10.cloned.1.call-done) | copy-start | bytes 9437188
  346.8 19.0 %copy-start.2 = (bf16[512,3072]{1,0:T(8,128)(2,1)S(1)}, bf16[512,3072]{1,0:T(8,128)(2,1)}, u32[]{:S(2)}) copy-start(bf16[512,3072]{1,0:T(8,128)(2,1)} %all-gather.6.cloned.1.call-done) | copy-start | bytes 9437188
  365.8 11.0 %copy-start = (bf16[1,64,1536]{2,1,0:T(8,128)(2,1)S(1)}, bf16[1,64,1536]{2,1,0:T(8,128)(2,1)}, u32[]{:S(2)}) copy-start(bf16[1,64,1536]{2,1,0:T(8,128)(2,1)} %param.5) | copy-start | bytes 589828
  365.8 41.4 %copy-start.1 = (bf16[1,64,1536]{2,1,0:T(8,128)(2,1)S(1)}, bf16[1,64,1536]{2,1,0:T(8,128)(2,1)}, u32[]{:S(2)}) copy-start(bf16[1,64,1536]{2,1,0:T(8,128)(2,1)} %param.8) | copy-start | bytes 589828
Sparse Core Ops, SparseCore 0:
  11.7 28.2 all-gather.7
  41.9 25.5 all-gather.11
  70.4 60.3 reduce-scatter.8
  133.5 60.3 reduce-scatter.4
  197.7 63.3 all-gather.5
  263.1 62.0 all-gather.9
  328.5 36.9 reduce-scatter.6
  368.8 38.3 reduce-scatter.10
